TPU v7x, 32 devices: a whole 2x2x4 slice. The times are simulated.
32 devices in a mesh: groups: 2 (over y), chan: 4 (over z), blk: 2 (over x), dir: 2 (over core).
Axes of the slice: x: 2, y: 2, z: 4, core: 2. Of those that a mesh axis runs over, the one named last changes fastest.
Arguments:
- visibilities: float32 [16, 8, 2, 512], P('groups', 'chan', 'blk'), parts along dimension 0, may hold values from -6 to 6
- antenna_pairs: int32 [2, 2, 512], P(None, 'blk'), may hold values from 0 to 511, as said below
- valid_mask: int32 [2, 1024], P('blk', 'groups'), parts along dimension 1, may hold values 0 or 1
- station_positions: float32 [2, 512], replicated, may hold values from -20 to 20
- source_offsets: float32 [2, 256], replicated, may hold values from -0.3 to 0.3
- brightness: float32 [4, 256], replicated, may hold values from -0.375 to 0.375
- source_cluster: int32 [256], replicated, may hold values from 0 to 15
- jones_gains: float32 [16, 16, 512], P('dir', 'groups'), parts along dimension 1, may hold values from -3 to 3
Outputs:
- residuals: float32 [16, 8, 2, 512], P('groups', None, 'blk', 'chan'), parts along dimension 0
- solved_gains: float32 [16, 16, 512], P('dir', 'groups'), parts along dimension 1
There are 2 independent parts, one for each index of `groups`. A program takes and returns all parts, laid end to end along the dimension named above; an argument that names none is the same for every part. Nothing has to cross between parts.
Inputs may be any that keep to these rules, and one draw needn't show every extreme that they name: `antenna_pairs`: the two stations of a baseline differ.
All inputs are finite; a program needn't handle non-finite values. No bound on the sum of `valid_mask` on one device may be relied on, other than what follows from the above.
Results may differ from a plain program's by a relative error of at most 0.0003.
Values sent between devices are 32-bit elements; how exact they have to be, the bound alone decides.
No kernel may reach another device: no remote copies, remote signals or barrier semaphores. Data moves between devices by JAX's collectives and lax.ppermute only.
A program may use at most 64 MiB of HBM per device.

v0:
```python
import math
import jax
import jax.numpy as jnp
from jax import lax
from jax.sharding import PartitionSpec as P

ITERS = 2
TWO_PI = 2.0 * math.pi
STEP_SIZE = 0.3
EPSILON = 1e-06
HIGHEST = lax.Precision.HIGHEST


def jones_product(former, latter):
    real_list = []
    imag_list = []
    for row_number in (0, 1):
        for column in (0, 1):
            real_list.append(
                former[2 * row_number] * latter[column]
                - former[4 + 2 * row_number] * latter[4 + column]
                + former[2 * row_number + 1] * latter[2 + column]
                - former[5 + 2 * row_number] * latter[6 + column]
            )
            imag_list.append(
                former[2 * row_number] * latter[4 + column]
                + former[4 + 2 * row_number] * latter[column]
                + former[2 * row_number + 1] * latter[6 + column]
                + former[5 + 2 * row_number] * latter[2 + column]
            )
    return jnp.stack(real_list + imag_list)


def adjoint(matrix):
    return jnp.stack(
        [matrix[0], matrix[2], matrix[1], matrix[3], -matrix[4], -matrix[6], -matrix[5], -matrix[7]]
    )


def source_table(brightness, source_cluster, direction_ids):
    member = (source_cluster[None, :] == direction_ids[:, None]).astype(jnp.float32)
    return (brightness[:, None, :] * member[None, :, :]).reshape(
        4 * direction_ids.shape[0], brightness.shape[1]
    )


def coherency(bright_table, geometry, scales):
    phase_grid = (TWO_PI * scales)[None, :, None] * geometry[:, None, :]
    phases_flat = phase_grid.reshape(geometry.shape[0], -1)
    real_block = jnp.dot(bright_table, jnp.cos(phases_flat), precision=HIGHEST)
    imag_block = -jnp.dot(bright_table, jnp.sin(phases_flat), precision=HIGHEST)
    dir_count = bright_table.shape[0] // 4
    return jnp.concatenate([real_block, imag_block], axis=0).reshape(
        8, dir_count, scales.shape[0], geometry.shape[1]
    )


def per_device(
    visibilities,
    antenna_pairs,
    valid_mask,
    station_positions,
    source_offsets,
    brightness,
    source_cluster,
    jones_gains,
):
    relay_count = lax.axis_size("chan")
    base_count = antenna_pairs.shape[2] // relay_count
    station_count = station_positions.shape[1]
    offset = lax.axis_index("chan") * base_count
    own_pairs = lax.dynamic_slice_in_dim(antenna_pairs[:, 0], offset, base_count, 1)
    first_station = own_pairs[0]
    second_station = own_pairs[1]
    weight_row = lax.dynamic_slice_in_dim(valid_mask[0], offset, base_count, 0).astype(jnp.float32)
    regrouped = lax.all_to_all(visibilities, "chan", split_axis=3, concat_axis=1, tiled=True)[
        :, :, 0, :
    ]
    total_channels = regrouped.shape[1]
    own_directions = jones_gains.shape[0]
    channel_ids = jnp.arange(total_channels)
    gains_now = jones_gains
    direction_ids = lax.axis_index("dir") * own_directions + jnp.arange(own_directions)
    local_channels = regrouped.shape[1]
    scales = 1.0 + 0.5 * channel_ids.astype(jnp.float32) / total_channels
    u_coord = station_positions[0][first_station] - station_positions[0][second_station]
    v_coord = station_positions[1][first_station] - station_positions[1][second_station]
    geometry = (
        source_offsets[0][:, None] * u_coord[None, :]
        + source_offsets[1][:, None] * v_coord[None, :]
    )
    bright_table = source_table(brightness, source_cluster, direction_ids)
    group_size = math.gcd(local_channels, max(1, 2048 // base_count))
    group_count = local_channels // group_size
    scale_groups = scales.reshape(group_count, group_size)
    onehot_first = (first_station[:, None] == jnp.arange(station_count)[None, :]).astype(
        jnp.float32
    )
    onehot_second = (second_station[:, None] == jnp.arange(station_count)[None, :]).astype(
        jnp.float32
    )

    def station_gains(gains_current):
        gain_first = jnp.take(gains_current, first_station, axis=2).transpose(1, 0, 2)[
            :, :, None, :
        ]
        gain_second = jnp.take(gains_current, second_station, axis=2).transpose(1, 0, 2)[
            :, :, None, :
        ]
        return (gain_first, gain_second)

    def residual_of(gains_current):
        gain_first, gain_second = station_gains(gains_current)

        def residual_one_group(scale_group):
            coherent = coherency(bright_table, geometry, scale_group)
            return jnp.sum(
                jones_product(jones_product(gain_first, coherent), adjoint(gain_second)), axis=1
            )

        partial_model = jnp.moveaxis(lax.map(residual_one_group, scale_groups), 0, 1).reshape(
            8, local_channels, base_count
        )
        model_vis = lax.psum(partial_model, "dir")
        return weight_row * (regrouped - model_vis)

    for iteration in range(ITERS):
        residual_now = residual_of(gains_now)
        updated_gain_first, updated_gain_second = station_gains(gains_now)
        resid_groups = jnp.moveaxis(
            residual_now.reshape(8, group_count, group_size, base_count), 1, 0
        )
        dir_count = gains_now.shape[0]

        def updated_one_group(running, inputs):
            scale_group, resid_group = inputs
            coherent = coherency(bright_table, geometry, scale_group)
            toward_second = jones_product(updated_gain_second, adjoint(coherent))
            toward_first = jones_product(updated_gain_first, coherent)
            grad_first = jnp.sum(jones_product(resid_group[:, None], toward_second), axis=2)
            grad_second = jnp.sum(
                jones_product(adjoint(resid_group)[:, None], toward_first), axis=2
            )
            curv_first = jnp.sum(toward_second * toward_second, axis=(0, 2))
            curv_second = jnp.sum(toward_first * toward_first, axis=(0, 2))
            return (
                (
                    running[0] + grad_first,
                    running[1] + grad_second,
                    running[2] + curv_first,
                    running[3] + curv_second,
                ),
                None,
            )

        zero_sums = (
            jnp.zeros((8, dir_count, base_count), jnp.float32),
            jnp.zeros((8, dir_count, base_count), jnp.float32),
            jnp.zeros((dir_count, base_count), jnp.float32),
            jnp.zeros((dir_count, base_count), jnp.float32),
        )
        totals, ignored = lax.scan(updated_one_group, zero_sums, (scale_groups, resid_groups))
        grad_station = jnp.einsum(
            "cdb,bs->dcs", totals[0], onehot_first, precision=HIGHEST
        ) + jnp.einsum("cdb,bs->dcs", totals[1], onehot_second, precision=HIGHEST)
        curv_station = jnp.dot(weight_row * totals[2], onehot_first, precision=HIGHEST) + jnp.dot(
            weight_row * totals[3], onehot_second, precision=HIGHEST
        )
        grad_station, curv_station = lax.psum((grad_station, curv_station), ("chan", "blk"))
        gains_now = gains_now + STEP_SIZE * grad_station / (curv_station[:, None, :] + EPSILON)
    residual_now = residual_of(gains_now)
    return (residual_now[:, :, None, :], gains_now)


def solution(mesh):
    in_specs = (
        P("groups", "chan", "blk", None),
        P(None, "blk", None),
        P("blk", "groups"),
        P(),
        P(),
        P(),
        P(),
        P("dir", "groups", None),
    )
    out_specs = (P("groups", None, "blk", "chan"), P("dir", "groups", None))
    return jax.shard_map(
        per_device, mesh=mesh, in_specs=in_specs, out_specs=out_specs, check_vma=False
    )
```

profile of v0, /device:TPU:0, one launch (start us, length us, event | category | flops | bytes accessed | tf_op | source)
XLA Modules:
  0.0 311.1 jit_solution(10712981869981205140)
XLA Ops:
  7.2 1.0 copy.374
  8.2 1.4 reshape.6361
  9.6 6.3 %all-to-all-start = ((f32[4,1,2048]{2,1,0:T(1,128)}), f32[4,1,2048]{2,1,0:T(1,128)S(1)}, u32[]{:S(2)}, u32[]{:S(2)}) async-start(f32[4,1,2048]{2,1,0:T(1,128)} %reshape.6361), calls=%async_computation | async-start | bytes 65536 | tf_op jit(solution)/shard_map/all_to_all | solution.py:76
  15.9 0.7 compare_and_fusion
  16.6 0.7 fusion.48
  17.3 0.8 fusion.56
  18.0 1.3 gather_fusion.3
  19.3 1.3 gather_fusion.1
  20.6 1.3 gather_fusion
  21.9 1.4 gather_fusion.2
  23.4 0.7 fusion.46
  24.4 3.7 %multiply_cosine_fusion = (f32[256,8,128]{2,1,0:T(8,128)S(1)}, f32[256,8,128]{2,1,0:T(8,128)S(1)}) fusion(f32[256,128]{1,0:T(8,128)S(1)} %multiply_add_fusion, f32[8]{0:T(128)S(1)} %add_multiply_fusion), kind=kLoop, calls=%fused_computation.11 | loop fusion | flops 262144 | bytes 2228256 | tf_op jit(solution)/shard_map/while/body/eval_jaxpr/cos | solution.py:50
  28.1 0.8 fusion.4
  28.9 0.8 convolution_negate_fusion
  29.7 0.7 copy.377
  30.5 0.8 gather_fusion.5
  31.3 1.6 gather_fusion.4
  33.0 2.0 fusion.55
  35.0 1.2 copy.387
  36.2 1.2 copy.390
  39.1 2.0 fusion.54
  41.1 1.2 copy.391
  42.3 1.2 copy.394
  46.2 37.6 %psum.51 = f32[8,512]{1,0:T(8,128)S(1)} all-reduce(f32[8,512]{1,0:T(8,128)S(1)} %convolution_add_fusion.3), channel_id=1, replica_groups=mesh['groups'=2,'chan'=4,'blk'=2,'dir'=2] {'chan','blk'}, use_global_device_ids=true, to_apply=%region_7.9 | all-reduce | flops 4096 | bytes 32768 | tf_op jit(solution)/shard_map/psum | solution.py:169
  83.7 3.6 %psum.49 = f32[8,8,128]{2,1,0:T(8,128)S(1)} all-reduce(f32[8,8,128]{2,1,0:T(8,128)S(1)} %reduce_sum.110), channel_id=1, replica_groups=mesh['groups'=2,'chan'=4,'blk'=2,'dir'=2] {'dir'}, use_global_device_ids=true, to_apply=%region_1.3 | all-reduce | flops 8192 | bytes 65536 | tf_op jit(solution)/shard_map/psum | solution.py:124
  87.4 0.5 broadcast.6420
  87.9 0.7 reduce
  88.6 0.8 reshape.6362
  89.7 0.5 copy-done.3
  90.7 0.3 fusion.15
  91.0 1.0 fusion.1
  92.0 67.1 %all-reduce.3.cloned.1.call-done = f32[8,8,512]{2,0,1:T(8,128)} async-done(((f32[8,8,512]{2,0,1:T(8,128)}), f32[8,8,512]{2,0,1:T(8,128)}) %all-reduce.3.cloned.1.call-update) | async-done | bytes 131088 | tf_op jit(solution)/shard_map/psum | solution.py:169
  159.1 1.0 copy_add_fusion
  160.1 0.8 copy.397
  160.9 0.8 gather_fusion.7
  161.7 0.8 gather_fusion.6
  162.9 2.1 fusion.53
  165.0 1.2 copy.407
  166.3 1.2 copy.410
  167.5 0.6 bitcast_negate_fusion
  168.1 1.2 copy.408
  169.3 0.6 bitcast_negate_fusion.1
  170.2 0.6 bitcast_negate_fusion.2
  171.0 0.6 bitcast_negate_fusion.3
  172.3 2.2 fusion.52
  174.4 1.2 copy.411
  175.7 1.2 copy.414
  176.9 1.2 copy.413
  180.1 0.7 constant_dynamic-update-slice_fusion.72
  181.1 35.4 %psum.54 = f32[8,512]{1,0:T(8,128)S(1)} all-reduce(f32[8,512]{1,0:T(8,128)S(1)} %convolution_add_fusion.2), channel_id=1, replica_groups=mesh['groups'=2,'chan'=4,'blk'=2,'dir'=2] {'chan','blk'}, use_global_device_ids=true, to_apply=%region_15.17 | all-reduce | flops 4096 | bytes 32768 | tf_op jit(solution)/shard_map/psum | solution.py:169
  216.8 3.7 %psum.52 = f32[8,8,128]{2,1,0:T(8,128)S(1)} all-reduce(f32[8,8,128]{2,1,0:T(8,128)S(1)} %reduce_sum.115), channel_id=1, replica_groups=mesh['groups'=2,'chan'=4,'blk'=2,'dir'=2] {'dir'}, use_global_device_ids=true, to_apply=%region_9.11 | all-reduce | flops 8192 | bytes 65536 | tf_op jit(solution)/shard_map/psum | solution.py:124
  221.0 0.3 fusion.13
  221.3 1.0 fusion
  222.3 67.1 %all-reduce.5.cloned.1.call-done = f32[8,8,512]{2,0,1:T(8,128)} async-done(((f32[8,8,512]{2,0,1:T(8,128)}), f32[8,8,512]{2,0,1:T(8,128)}) %all-reduce.5.cloned.1.call-update) | async-done | bytes 131088 | tf_op jit(solution)/shard_map/psum | solution.py:169
  289.4 0.9 divide_add_fusion
  290.4 0.7 copy.429
  291.1 0.8 copy.416
  291.9 0.9 gather_fusion.9
  292.8 0.9 gather_fusion.8
  294.1 2.0 fusion.51
  296.1 1.2 copy.423
  297.3 1.2 copy.426
  300.2 3.4 %psum.55 = f32[8,8,128]{2,1,0:T(8,128)S(1)} all-reduce(f32[8,8,128]{2,1,0:T(8,128)S(1)} %reduce_sum.120), channel_id=1, replica_groups=mesh['groups'=2,'chan'=4,'blk'=2,'dir'=2] {'dir'}, use_global_device_ids=true, to_apply=%region_17.19 | all-reduce | flops 8192 | bytes 65536 | tf_op jit(solution)/shard_map/psum | solution.py:124
  303.7 0.6 subtract_multiply_fusion
  (228 shorter events, 11.5 us)
Async XLA Ops:
  7.2 16.9 %copy-start.32 = (f32[2,256]{1,0:T(2,128)S(1)}, f32[2,256]{1,0:T(2,128)}, u32[]{:S(2)}) copy-start(f32[2,256]{1,0:T(2,128)} %param.14) | copy-start | bytes 6148
  7.2 17.0 %copy-start.37 = (s32[256]{0:T(256)S(1)}, s32[256]{0:T(256)}, u32[]{:S(2)}) copy-start(s32[256]{0:T(256)} %param.16) | copy-start | bytes 3076
  9.6 77.8 %all-to-all-start = ((f32[4,1,2048]{2,1,0:T(1,128)}), f32[4,1,2048]{2,1,0:T(1,128)S(1)}, u32[]{:S(2)}, u32[]{:S(2)}) async-start(f32[4,1,2048]{2,1,0:T(1,128)} %reshape.6361), calls=%async_computation | async-start | bytes 65536 | tf_op jit(solution)/shard_map/all_to_all | solution.py:76
  15.9 143.2 %all-reduce.3.cloned.1.call-start = ((), (), s32[]{:S(2)}) async-start(), calls=%async_computation.1 | async-start | bytes 262144 | tf_op jit(solution)/shard_map/psum | solution.py:169
  16.6 74.1 %copy-start.35 = (s32[128]{0:T(128)}, s32[128]{0:T(128)S(1)}, u32[]{:S(2)}) copy-start(s32[128]{0:T(128)S(1)} %get-tuple-element.223) | copy-start | bytes 1540
  16.6 145.9 %copy-start.23 = (pred[128]{0:T(512)(128)(4,1)}, pred[128]{0:T(512)(128)(4,1)S(1)}, u32[]{:S(2)}) copy-start(pred[128]{0:T(512)(128)(4,1)S(1)} %get-tuple-element.222) | copy-start | bytes 388
  17.3 73.7 %copy-start.33 = (s32[1,1,128]{2,1,0:T(1,128)}, s32[1,1,128]{2,1,0:T(1,128)S(1)}, u32[]{:S(2)}) copy-start(s32[1,1,128]{2,1,0:T(1,128)S(1)} %get-tuple-element.225) | copy-start | bytes 1540
  19.3 8.7 %copy-start.22 = (f32[4,256]{1,0:T(4,128)S(1)}, f32[4,256]{1,0:T(4,128)}, u32[]{:S(2)}) copy-start(f32[4,256]{1,0:T(4,128)} %param.15) | copy-start | bytes 12292
  24.0 65.6 %copy-start.27 = (f32[128]{0:T(128)}, f32[128]{0:T(128)S(1)}, u32[]{:S(2)}) copy-start(f32[128]{0:T(128)S(1)} %fusion.46) | copy-start | bytes 1540
  24.0 138.7 %copy-start.30 = (pred[128]{0:T(512)(128)(4,1)}, pred[128]{0:T(512)(128)(4,1)S(1)}, u32[]{:S(2)}) copy-start(pred[128]{0:T(512)(128)(4,1)S(1)} %compare_and_fusion.1) | copy-start | bytes 388
  24.1 137.6 %copy-start.25 = (s32[1024]{0:T(1024)}, s32[1024]{0:T(1024)S(1)}, u32[]{:S(2)}) copy-start(s32[1024]{0:T(1024)S(1)} %pad_clamp_fusion.3) | copy-start | bytes 12292
  24.1 136.8 %copy-start.26 = (s32[1024]{0:T(1024)}, s32[1024]{0:T(1024)S(1)}, u32[]{:S(2)}) copy-start(s32[1024]{0:T(1024)S(1)} %pad_clamp_fusion) | copy-start | bytes 12292
  24.4 5.4 %copy-start.1 = (f32[8,8,512]{2,1,0:T(8,128)S(1)}, f32[8,8,512]{2,1,0:T(8,128)}, u32[]{:S(2)}) copy-start(f32[8,8,512]{2,1,0:T(8,128)} %param.17) | copy-start | bytes 393220
  37.7 1.2 copy-start
  89.6 0.6 copy-start.3
  90.3 68.9 %copy-start.2 = (f32[8,8,512]{2,1,0:T(8,128)S(1)}, f32[8,8,512]{2,1,0:T(8,128)}, u32[]{:S(2)}) copy-start(f32[8,8,512]{2,1,0:T(8,128)} %param.17) | copy-start | bytes 393220
  91.9 197.5 %all-reduce.5.cloned.1.call-start = ((), (), s32[]{:S(2)}) async-start(), calls=%async_computation.2 | async-start | bytes 262144 | tf_op jit(solution)/shard_map/psum | solution.py:169
  167.5 4.1 %copy-start.6 = (f32[1,8,128]{2,1,0:T(8,128)}, f32[1,8,128]{2,1,0:T(8,128)S(1)}, u32[]{:S(2)}) copy-start(f32[1,8,128]{2,1,0:T(8,128)S(1)} %copy.410) | copy-start | bytes 12292
  169.3 2.5 copy-start.8
  170.2 1.9 copy-start.10
  171.0 1.1 copy-start.12
  174.4 4.9 %copy-start.11 = (f32[1,8,128]{2,1,0:T(8,128)S(1)}, f32[1,8,128]{2,1,0:T(8,128)}, u32[]{:S(2)}) copy-start(f32[1,8,128]{2,1,0:T(8,128)} %copy-done.10) | copy-start | bytes 12292
  174.4 4.9 %copy-start.13 = (f32[1,8,128]{2,1,0:T(8,128)S(1)}, f32[1,8,128]{2,1,0:T(8,128)}, u32[]{:S(2)}) copy-start(f32[1,8,128]{2,1,0:T(8,128)} %copy-done.12) | copy-start | bytes 12292
  175.7 4.4 %copy-start.14 = (f32[1,8,128]{2,1,0:T(8,128)}, f32[1,8,128]{2,1,0:T(8,128)S(1)}, u32[]{:S(2)}) copy-start(f32[1,8,128]{2,1,0:T(8,128)S(1)} %copy.411) | copy-start | bytes 12292
  176.9 3.1 %copy-start.15 = (f32[1,8,128]{2,1,0:T(8,128)}, f32[1,8,128]{2,1,0:T(8,128)S(1)}, u32[]{:S(2)}) copy-start(f32[1,8,128]{2,1,0:T(8,128)S(1)} %copy.414) | copy-start | bytes 12292
  176.9 2.5 copy-start.7
  176.9 2.5 copy-start.9
  178.2 1.9 copy-start.16
  178.4 1.7 copy-start.17
  178.6 1.1 copy-start.28
  178.6 1.1 copy-start.36
  179.1 1.8 copy-start.34
  179.3 37.3 %copy-start.20 = (f32[8,128]{1,0:T(8,128)S(1)}, f32[8,128]{1,0:T(8,128)}, u32[]{:S(2)}) copy-start(f32[8,128]{1,0:T(8,128)} %bitcast_negate_fusion.2) | copy-start | bytes 12292
  179.3 37.3 %copy-start.21 = (f32[8,128]{1,0:T(8,128)S(1)}, f32[8,128]{1,0:T(8,128)}, u32[]{:S(2)}) copy-start(f32[8,128]{1,0:T(8,128)} %bitcast_negate_fusion.3) | copy-start | bytes 12292
  179.3 37.3 %copy-start.18 = (f32[8,128]{1,0:T(8,128)S(1)}, f32[8,128]{1,0:T(8,128)}, u32[]{:S(2)}) copy-start(f32[8,128]{1,0:T(8,128)} %bitcast_negate_fusion) | copy-start | bytes 12292
  179.3 37.3 %copy-start.19 = (f32[8,128]{1,0:T(8,128)S(1)}, f32[8,128]{1,0:T(8,128)}, u32[]{:S(2)}) copy-start(f32[8,128]{1,0:T(8,128)} %bitcast_negate_fusion.1) | copy-start | bytes 12292
  179.5 41.0 %copy-start.4 = (f32[8,4,2,1,128]{4,0,2,1,3:T(8,128)S(1)}, f32[8,4,2,1,128]{4,0,2,1,3:T(8,128)}, u32[]{:S(2)}) copy-start(f32[8,4,2,1,128]{4,0,2,1,3:T(8,128)} %copy-done.3) | copy-start | bytes 98308
  221.3 72.5 %copy-start.31 = (pred[128]{0:T(512)(128)(4,1)S(1)}, pred[128]{0:T(512)(128)(4,1)}, u32[]{:S(2)}) copy-start(pred[128]{0:T(512)(128)(4,1)} %copy-done.30) | copy-start | bytes 388
  221.3 72.6 %copy-start.24 = (pred[128]{0:T(512)(128)(4,1)S(1)}, pred[128]{0:T(512)(128)(4,1)}, u32[]{:S(2)}) copy-start(pred[128]{0:T(512)(128)(4,1)} %copy-done.23) | copy-start | bytes 388
  299.2 4.5 %copy-start.5 = (f32[8,4,2,1,128]{4,0,2,1,3:T(8,128)S(1)}, f32[8,4,2,1,128]{4,0,2,1,3:T(8,128)}, u32[]{:S(2)}) copy-start(f32[8,4,2,1,128]{4,0,2,1,3:T(8,128)} %copy-done.3) | copy-start | bytes 98308
  299.2 4.5 %copy-start.29 = (f32[128]{0:T(128)S(1)}, f32[128]{0:T(128)}, u32[]{:S(2)}) copy-start(f32[128]{0:T(128)} %copy-done.27) | copy-start | bytes 1540
Sparse Core Ops, SparseCore 0:
  92.1 67.0 all-reduce.2
  222.4 66.9 all-reduce.4
where the time goes:
time: 312 us; the launch traced here: 311 us
  waiting for transfers between devices  134 us (43%)
  blocking collectives  83.7 us (27%)
  local copies, waits for them, and re-layouts  50.7 us (16%)
  other arithmetic  15.7 us (5%)
  between operations  15.3 us (5%)
  starting transfers between devices  6.36 us (2%)
  matrix products  5.15 us (2%)
    psum x2, waiting for transfers between devices, per_device(): lax.psum((grad_station, curv_station), ('chan', 'blk'))  134 us
    psum x2, blocking collectives, per_device(): lax.psum((grad_station, curv_station), ('chan', 'blk'))  73 us
    psum x3, blocking collectives, residual_of(): model_vis = lax.psum(partial_model, 'dir')  10.7 us
    slice x9, local copies, waits for them, and re-layouts, jones_product(): former[2 * row_number] * latter[column]  10.5 us
    slice x4, local copies, waits for them, and re-layouts, adjoint(): matrix[2]  6.6 us
    all_to_all x1, starting transfers between devices, per_device(): lax.all_to_all(visibilities, 'chan', split_axis=3, concat_axis=1, tiled=T...  6.32 us
  transfers between devices with their start and end apart: 3, of which 2 were waited for; matrix products, arithmetic and copies ran while one was open for 10% of the time, Pallas kernels for 0%

commit v1 on v0

--- a/solution.py
+++ b/solution.py
@@ -166,7 +166,7 @@
         curv_station = jnp.dot(weight_row * totals[2], onehot_first, precision=HIGHEST) + jnp.dot(
             weight_row * totals[3], onehot_second, precision=HIGHEST
         )
-        grad_station, curv_station = lax.psum((grad_station, curv_station), ("chan", "blk"))
+        grad_station, curv_station = lax.psum(lax.psum((grad_station, curv_station), "blk"), "chan")
         gains_now = gains_now + STEP_SIZE * grad_station / (curv_station[:, None, :] + EPSILON)
     residual_now = residual_of(gains_now)
     return (residual_now[:, :, None, :], gains_now)

time: 312 us -> 222 us (0.71)
  waiting for transfers between devices: 134 us -> 64.2 us
  blocking collectives: 83.7 us -> 63.4 us
    psum x2 -> x4, waiting for transfers between devices: 134 us -> 64.2 us  [the longest x2 64.2 us: per_device(): lax.psum(lax.psum((grad_station, curv_station), 'blk'), 'chan')]
    psum x2 -> x4, blocking collectives: 73 us -> 53 us  [the longest x2 36.7 us: per_device(): lax.psum(lax.psum((grad_station, curv_station), 'blk'), 'chan')]
  transfers between devices with their start and end apart: 3 -> 5, of which waited for: 2 -> 2; matrix products, arithmetic and copies ran while one was open for 10% -> 14% of each run, Pallas kernels for 0% -> 0%
where the time goes in v1:
time: 222 us; the launch traced here: 221 us
  waiting for transfers between devices  64.2 us (29%)
  blocking collectives  63.4 us (29%)
  local copies, waits for them, and re-layouts  50.8 us (23%)
  other arithmetic  15.7 us (7%)
  between operations  15 us (7%)
  starting transfers between devices  6.44 us (3%)
  matrix products  5.15 us (2%)
    psum x2, waiting for transfers between devices, per_device(): lax.psum(lax.psum((grad_station, curv_station), 'blk'), 'chan')  64.2 us
    psum x2, blocking collectives, per_device(): lax.psum(lax.psum((grad_station, curv_station), 'blk'), 'chan')  36.7 us
    psum x2, blocking collectives, per_device(): lax.psum((grad_station, curv_station), 'blk')  16.3 us
    slice x9, local copies, waits for them, and re-layouts, jones_product(): former[2 * row_number] * latter[column]  10.6 us
    psum x3, blocking collectives, residual_of(): model_vis = lax.psum(partial_model, 'dir')  10.4 us
    slice x4, local copies, waits for them, and re-layouts, adjoint(): matrix[2]  6.63 us
    all_to_all x1, starting transfers between devices, per_device(): lax.all_to_all(visibilities, 'chan', split_axis=3, concat_axis=1, tiled=T...  6.32 us
    unnamed x81, local copies, waits for them, and re-layouts  5.33 us
  transfers between devices with their start and end apart: 5, of which 2 were waited for; matrix products, arithmetic and copies ran while one was open for 14% of the time, Pallas kernels for 0%

profile of v1, /device:TPU:0, one launch (start us, length us, event | category | flops | bytes accessed | tf_op | source)
XLA Modules:
  0.0 220.7 jit_solution(4735894076862289247)
XLA Ops:
  7.2 1.0 copy.374
  8.2 1.4 reshape.6361
  9.6 6.3 %all-to-all-start = ((f32[4,1,2048]{2,1,0:T(1,128)}), f32[4,1,2048]{2,1,0:T(1,128)S(1)}, u32[]{:S(2)}, u32[]{:S(2)}) async-start(f32[4,1,2048]{2,1,0:T(1,128)} %reshape.6361), calls=%async_computation | async-start | bytes 65536 | tf_op jit(solution)/shard_map/all_to_all | solution.py:76
  15.9 0.7 compare_and_fusion
  16.6 0.7 fusion.48
  17.3 0.8 fusion.56
  18.0 1.3 gather_fusion.3
  19.3 1.3 gather_fusion.1
  20.6 1.3 gather_fusion
  21.9 1.4 gather_fusion.2
  23.4 0.7 fusion.46
  24.4 3.7 %multiply_cosine_fusion = (f32[256,8,128]{2,1,0:T(8,128)S(1)}, f32[256,8,128]{2,1,0:T(8,128)S(1)}) fusion(f32[256,128]{1,0:T(8,128)S(1)} %multiply_add_fusion, f32[8]{0:T(128)S(1)} %add_multiply_fusion), kind=kLoop, calls=%fused_computation.11 | loop fusion | flops 262144 | bytes 2228256 | tf_op jit(solution)/shard_map/while/body/eval_jaxpr/cos | solution.py:50
  28.1 0.8 fusion.4
  28.9 0.8 convolution_negate_fusion
  29.7 0.7 copy.377
  30.5 0.8 gather_fusion.5
  31.3 1.6 gather_fusion.4
  33.0 2.0 fusion.55
  35.0 1.2 copy.387
  36.3 1.2 copy.390
  39.1 2.0 fusion.54
  41.1 1.2 copy.391
  42.3 1.2 copy.394
  45.9 3.6 %psum.77 = f32[8,8,128]{2,1,0:T(8,128)S(1)} all-reduce(f32[8,8,128]{2,1,0:T(8,128)S(1)} %reduce_sum.110), channel_id=1, replica_groups=mesh['groups'=2,'chan'=4,'blk'=2,'dir'=2] {'dir'}, use_global_device_ids=true, to_apply=%region_1.3 | all-reduce | flops 8192 | bytes 65536 | tf_op jit(solution)/shard_map/psum | solution.py:124
  49.6 0.5 broadcast.6420
  50.1 0.7 reduce
  50.8 0.8 reshape.6362
  52.0 0.5 copy-done.3
  53.1 1.0 fusion.1
  54.4 8.1 %psum.80 = f32[8,512]{1,0:T(8,128)S(1)} all-reduce(f32[8,512]{1,0:T(8,128)S(1)} %convolution_add_fusion.3), channel_id=1, replica_groups=mesh['groups'=2,'chan'=4,'blk'=2,'dir'=2] {'blk'}, use_global_device_ids=true, to_apply=%region_8.10 | all-reduce | flops 4096 | bytes 32768 | tf_op jit(solution)/shard_map/psum | solution.py:169
  62.6 19.2 %psum.81 = f32[8,512]{1,0:T(8,128)S(1)} all-reduce(f32[8,512]{1,0:T(8,128)S(1)} %psum.80), channel_id=1, replica_groups=mesh['groups'=2,'chan'=4,'blk'=2,'dir'=2] {'chan'}, use_global_device_ids=true, to_apply=%region_9.11 | all-reduce | flops 4096 | bytes 32768 | tf_op jit(solution)/shard_map/psum | solution.py:169
  81.9 32.1 %all-reduce.7.cloned.1.call-done = f32[8,8,512]{2,0,1:T(8,128)} async-done(((f32[8,8,512]{2,0,1:T(8,128)}), f32[8,8,512]{2,0,1:T(8,128)}) %all-reduce.7.cloned.1.call-update) | async-done | bytes 131088 | tf_op jit(solution)/shard_map/psum | solution.py:169
  113.9 1.0 copy_add_fusion
  114.9 0.8 copy.397
  115.7 0.8 gather_fusion.7
  116.5 0.8 gather_fusion.6
  117.7 2.2 fusion.53
  119.9 1.2 copy.407
  121.1 1.2 copy.410
  122.3 0.6 bitcast_negate_fusion
  122.9 1.2 copy.408
  124.2 0.6 bitcast_negate_fusion.1
  125.0 0.6 bitcast_negate_fusion.2
  125.8 0.6 bitcast_negate_fusion.3
  127.1 2.2 fusion.52
  129.3 1.2 copy.411
  130.5 1.2 copy.414
  131.8 1.2 copy.413
  134.9 0.7 constant_dynamic-update-slice_fusion.72
  136.0 3.4 %psum.82 = f32[8,8,128]{2,1,0:T(8,128)S(1)} all-reduce(f32[8,8,128]{2,1,0:T(8,128)S(1)} %reduce_sum.115), channel_id=1, replica_groups=mesh['groups'=2,'chan'=4,'blk'=2,'dir'=2] {'dir'}, use_global_device_ids=true, to_apply=%region_11.13 | all-reduce | flops 8192 | bytes 65536 | tf_op jit(solution)/shard_map/psum | solution.py:124
  140.2 1.0 fusion
  141.5 8.1 %psum.85 = f32[8,512]{1,0:T(8,128)S(1)} all-reduce(f32[8,512]{1,0:T(8,128)S(1)} %convolution_add_fusion.2), channel_id=1, replica_groups=mesh['groups'=2,'chan'=4,'blk'=2,'dir'=2] {'blk'}, use_global_device_ids=true, to_apply=%region_18.20 | all-reduce | flops 4096 | bytes 32768 | tf_op jit(solution)/shard_map/psum | solution.py:169
  149.7 17.5 %psum.86 = f32[8,512]{1,0:T(8,128)S(1)} all-reduce(f32[8,512]{1,0:T(8,128)S(1)} %psum.85), channel_id=1, replica_groups=mesh['groups'=2,'chan'=4,'blk'=2,'dir'=2] {'chan'}, use_global_device_ids=true, to_apply=%region_19.21 | all-reduce | flops 4096 | bytes 32768 | tf_op jit(solution)/shard_map/psum | solution.py:169
  167.2 32.1 %all-reduce.11.cloned.1.call-done = f32[8,8,512]{2,0,1:T(8,128)} async-done(((f32[8,8,512]{2,0,1:T(8,128)}), f32[8,8,512]{2,0,1:T(8,128)}) %all-reduce.11.cloned.1.call-update) | async-done | bytes 131088 | tf_op jit(solution)/shard_map/psum | solution.py:169
  199.3 0.9 divide_add_fusion
  200.2 0.7 copy.429
  201.0 0.8 copy.416
  201.7 0.9 gather_fusion.9
  202.6 0.9 gather_fusion.8
  204.0 2.0 fusion.51
  206.0 1.2 copy.423
  207.2 1.2 copy.426
  210.1 3.4 %psum.87 = f32[8,8,128]{2,1,0:T(8,128)S(1)} all-reduce(f32[8,8,128]{2,1,0:T(8,128)S(1)} %reduce_sum.120), channel_id=1, replica_groups=mesh['groups'=2,'chan'=4,'blk'=2,'dir'=2] {'dir'}, use_global_device_ids=true, to_apply=%region_21.23 | all-reduce | flops 8192 | bytes 65536 | tf_op jit(solution)/shard_map/psum | solution.py:124
  213.6 0.6 subtract_multiply_fusion
  (236 shorter events, 12.2 us)
Async XLA Ops:
  7.2 16.9 %copy-start.32 = (f32[2,256]{1,0:T(2,128)S(1)}, f32[2,256]{1,0:T(2,128)}, u32[]{:S(2)}) copy-start(f32[2,256]{1,0:T(2,128)} %param.14) | copy-start | bytes 6148
  7.2 17.0 %copy-start.37 = (s32[256]{0:T(256)S(1)}, s32[256]{0:T(256)}, u32[]{:S(2)}) copy-start(s32[256]{0:T(256)} %param.16) | copy-start | bytes 3076
  9.6 40.0 %all-to-all-start = ((f32[4,1,2048]{2,1,0:T(1,128)}), f32[4,1,2048]{2,1,0:T(1,128)S(1)}, u32[]{:S(2)}, u32[]{:S(2)}) async-start(f32[4,1,2048]{2,1,0:T(1,128)} %reshape.6361), calls=%async_computation | async-start | bytes 65536 | tf_op jit(solution)/shard_map/all_to_all | solution.py:76
  15.9 65.9 %all-reduce.5.cloned.1.call-start = ((), (), s32[]{:S(2)}) async-start(), calls=%async_computation.1 | async-start | bytes 262144 | tf_op jit(solution)/shard_map/psum | solution.py:169
  16.6 36.2 %copy-start.35 = (s32[128]{0:T(128)}, s32[128]{0:T(128)S(1)}, u32[]{:S(2)}) copy-start(s32[128]{0:T(128)S(1)} %get-tuple-element.223) | copy-start | bytes 1540
  16.6 100.7 %copy-start.23 = (pred[128]{0:T(512)(128)(4,1)}, pred[128]{0:T(512)(128)(4,1)S(1)}, u32[]{:S(2)}) copy-start(pred[128]{0:T(512)(128)(4,1)S(1)} %get-tuple-element.222) | copy-start | bytes 388
  17.3 36.9 %copy-start.33 = (s32[1,1,128]{2,1,0:T(1,128)}, s32[1,1,128]{2,1,0:T(1,128)S(1)}, u32[]{:S(2)}) copy-start(s32[1,1,128]{2,1,0:T(1,128)S(1)} %get-tuple-element.225) | copy-start | bytes 1540
  19.3 8.7 %copy-start.22 = (f32[4,256]{1,0:T(4,128)S(1)}, f32[4,256]{1,0:T(4,128)}, u32[]{:S(2)}) copy-start(f32[4,256]{1,0:T(4,128)} %param.15) | copy-start | bytes 12292
  24.0 30.2 %copy-start.27 = (f32[128]{0:T(128)}, f32[128]{0:T(128)S(1)}, u32[]{:S(2)}) copy-start(f32[128]{0:T(128)S(1)} %fusion.46) | copy-start | bytes 1540
  24.0 93.5 %copy-start.30 = (pred[128]{0:T(512)(128)(4,1)}, pred[128]{0:T(512)(128)(4,1)S(1)}, u32[]{:S(2)}) copy-start(pred[128]{0:T(512)(128)(4,1)S(1)} %compare_and_fusion.1) | copy-start | bytes 388
  24.1 92.4 %copy-start.25 = (s32[1024]{0:T(1024)}, s32[1024]{0:T(1024)S(1)}, u32[]{:S(2)}) copy-start(s32[1024]{0:T(1024)S(1)} %pad_clamp_fusion.3) | copy-start | bytes 12292
  24.1 91.6 %copy-start.26 = (s32[1024]{0:T(1024)}, s32[1024]{0:T(1024)S(1)}, u32[]{:S(2)}) copy-start(s32[1024]{0:T(1024)S(1)} %pad_clamp_fusion) | copy-start | bytes 12292
  24.4 5.4 %copy-start.1 = (f32[8,8,512]{2,1,0:T(8,128)S(1)}, f32[8,8,512]{2,1,0:T(8,128)}, u32[]{:S(2)}) copy-start(f32[8,8,512]{2,1,0:T(8,128)} %param.17) | copy-start | bytes 393220
  37.7 1.2 copy-start
  51.8 0.6 copy-start.3
  52.5 61.5 %copy-start.2 = (f32[8,8,512]{2,1,0:T(8,128)S(1)}, f32[8,8,512]{2,1,0:T(8,128)}, u32[]{:S(2)}) copy-start(f32[8,8,512]{2,1,0:T(8,128)} %param.17) | copy-start | bytes 393220
  54.1 59.8 %all-reduce.7.cloned.1.call-start = ((), (), s32[]{:S(2)}) async-start(), calls=%async_computation.2 | async-start | bytes 262144 | tf_op jit(solution)/shard_map/psum | solution.py:169
  81.8 85.3 %all-reduce.9.cloned.1.call-start = ((), (), s32[]{:S(2)}) async-start(), calls=%async_computation.3 | async-start | bytes 262144 | tf_op jit(solution)/shard_map/psum | solution.py:169
  122.3 4.1 %copy-start.6 = (f32[1,8,128]{2,1,0:T(8,128)}, f32[1,8,128]{2,1,0:T(8,128)S(1)}, u32[]{:S(2)}) copy-start(f32[1,8,128]{2,1,0:T(8,128)S(1)} %copy.410) | copy-start | bytes 12292
  124.2 2.5 %copy-start.8 = (f32[1,8,128]{2,1,0:T(8,128)}, f32[1,8,128]{2,1,0:T(8,128)S(1)}, u32[]{:S(2)}) copy-start(f32[1,8,128]{2,1,0:T(8,128)S(1)} %copy.408) | copy-start | bytes 12292
  125.0 1.9 copy-start.10
  125.8 1.1 copy-start.12
  129.3 4.9 %copy-start.11 = (f32[1,8,128]{2,1,0:T(8,128)S(1)}, f32[1,8,128]{2,1,0:T(8,128)}, u32[]{:S(2)}) copy-start(f32[1,8,128]{2,1,0:T(8,128)} %copy-done.10) | copy-start | bytes 12292
  129.3 4.9 %copy-start.13 = (f32[1,8,128]{2,1,0:T(8,128)S(1)}, f32[1,8,128]{2,1,0:T(8,128)}, u32[]{:S(2)}) copy-start(f32[1,8,128]{2,1,0:T(8,128)} %copy-done.12) | copy-start | bytes 12292
  130.5 4.3 %copy-start.14 = (f32[1,8,128]{2,1,0:T(8,128)}, f32[1,8,128]{2,1,0:T(8,128)S(1)}, u32[]{:S(2)}) copy-start(f32[1,8,128]{2,1,0:T(8,128)S(1)} %copy.411) | copy-start | bytes 12292
  131.8 3.1 %copy-start.15 = (f32[1,8,128]{2,1,0:T(8,128)}, f32[1,8,128]{2,1,0:T(8,128)S(1)}, u32[]{:S(2)}) copy-start(f32[1,8,128]{2,1,0:T(8,128)S(1)} %copy.414) | copy-start | bytes 12292
  131.8 2.5 %copy-start.7 = (f32[1,8,128]{2,1,0:T(8,128)S(1)}, f32[1,8,128]{2,1,0:T(8,128)}, u32[]{:S(2)}) copy-start(f32[1,8,128]{2,1,0:T(8,128)} %copy-done.6) | copy-start | bytes 12292
  131.8 2.5 %copy-start.9 = (f32[1,8,128]{2,1,0:T(8,128)S(1)}, f32[1,8,128]{2,1,0:T(8,128)}, u32[]{:S(2)}) copy-start(f32[1,8,128]{2,1,0:T(8,128)} %copy-done.8) | copy-start | bytes 12292
  133.0 1.9 copy-start.16
  133.2 1.7 copy-start.17
  133.5 1.1 copy-start.28
  133.5 1.1 copy-start.36
  133.9 1.8 copy-start.20
  133.9 1.8 copy-start.21
  134.2 1.6 copy-start.18
  134.2 1.6 copy-start.19
  134.4 5.1 %copy-start.4 = (f32[8,4,2,1,128]{4,0,2,1,3:T(8,128)S(1)}, f32[8,4,2,1,128]{4,0,2,1,3:T(8,128)}, u32[]{:S(2)}) copy-start(f32[8,4,2,1,128]{4,0,2,1,3:T(8,128)} %copy-done.3) | copy-start | bytes 98308
  139.4 0.8 copy-start.34
  141.2 62.5 %copy-start.31 = (pred[128]{0:T(512)(128)(4,1)S(1)}, pred[128]{0:T(512)(128)(4,1)}, u32[]{:S(2)}) copy-start(pred[128]{0:T(512)(128)(4,1)} %copy-done.30) | copy-start | bytes 388
  141.2 62.5 %copy-start.24 = (pred[128]{0:T(512)(128)(4,1)S(1)}, pred[128]{0:T(512)(128)(4,1)}, u32[]{:S(2)}) copy-start(pred[128]{0:T(512)(128)(4,1)} %copy-done.23) | copy-start | bytes 388
  141.2 58.1 %all-reduce.11.cloned.1.call-start = ((), (), s32[]{:S(2)}) async-start(), calls=%async_computation.4 | async-start | bytes 262144 | tf_op jit(solution)/shard_map/psum | solution.py:169
  209.1 4.5 %copy-start.5 = (f32[8,4,2,1,128]{4,0,2,1,3:T(8,128)S(1)}, f32[8,4,2,1,128]{4,0,2,1,3:T(8,128)}, u32[]{:S(2)}) copy-start(f32[8,4,2,1,128]{4,0,2,1,3:T(8,128)} %copy-done.3) | copy-start | bytes 98308
  209.1 4.5 %copy-start.29 = (f32[128]{0:T(128)S(1)}, f32[128]{0:T(128)}, u32[]{:S(2)}) copy-start(f32[128]{0:T(128)} %copy-done.27) | copy-start | bytes 1540
Sparse Core Ops, SparseCore 0:
  54.2 22.9 all-reduce.4
  81.9 31.9 all-reduce.6
  141.3 21.1 all-reduce.8
  167.3 31.9 all-reduce.10
